TPU v7x, 128 devices: a whole 4x4x4 slice. The times are simulated.
128 devices in a mesh: ctx: 32 (over z, x, core), tp: 4 (over y).
Axes of the slice: x: 4, y: 4, z: 4, core: 2. Of those that a mesh axis runs over, the one named last changes fastest.
Arguments:
- tokens: bfloat16 [4096, 4096], P('ctx', 'tp'), may hold values from -6 to 6
- in_weight: bfloat16 [4096, 3, 4096], P('ctx', None, 'tp'), may hold values from -0.09375 to 0.09375
- conv_taps: float32 [3, 3, 4096], P(None, None, 'tp'), may hold values from -2.5 to 2.5
- decay_rate: float32 [16, 4096], P(None, 'tp'), may hold values from 0 to 0.034, as said below
- residue: float32 [16, 4096], P(None, 'tp'), may hold values from -1 to 1
- skip: float32 [4096], P('tp'), may hold values from -1 to 1
Outputs:
- mixed: bfloat16 [4096, 4096], P('ctx', 'tp')
Inputs may be any that keep to these rules, and one draw needn't show every extreme that they name: `decay_rate`: positive decay rates of the poles.
All inputs are finite; a program needn't handle non-finite values.
Results may differ from a plain program's by a relative error of at most 0.0063.
Values may be sent and summed in bfloat16 or wider, within the bound.
A program may use at most 128 MiB of HBM per device.

v0:
```python
import math
import jax
import jax.numpy as jnp
from jax import lax
from jax.sharding import PartitionSpec as P


def passed_along(array, axis, by):
    peers = lax.axis_size(axis)
    pairs = [(i, i + by) for i in range(peers) if 0 <= i + by < peers]
    return lax.ppermute(array, axis, pairs)


def entering(array, axis, combine, identity):
    peers, here = (lax.axis_size(axis), lax.axis_index(axis))
    everything = jax.tree.map(lambda part: lax.all_gather(part, axis), array)
    start = jax.tree.map(
        lambda part, zero: jnp.broadcast_to(jnp.asarray(zero, part.dtype), part.shape),
        array,
        identity,
    )

    def turn(k, before):
        reached = k < here
        new = combine(before, jax.tree.map(lambda part: part[k], everything))
        return jax.tree.map(lambda a, b: jnp.where(reached, a, b), new, before)

    return lax.fori_loop(0, peers, turn, start)


def link(earlier, later):
    return (earlier[0] * later[0], later[0] * earlier[1] + later[1])


def per_device(tokens, in_weight, conv_taps, decay_rate, residue, skip):
    rows = tokens.shape[0]
    chans = in_weight.shape[2]
    whole = lax.all_gather(tokens, "tp", axis=1, tiled=True)
    piece = lax.all_gather(in_weight, "ctx", axis=0, tiled=True)
    sums = tuple(
        (jnp.dot(whole, piece[:, g, :], preferred_element_type=jnp.float32) for g in range(3))
    )
    projected = jnp.stack([total.astype(jnp.bfloat16) for total in sums], axis=0)
    edge_out = passed_along(projected[:, rows - 2 :, :], "ctx", 1)
    extended = jnp.concatenate([edge_out, projected], axis=1)
    values = lax.optimization_barrier(extended).astype(jnp.float32)
    filtered = (
        conv_taps[0][:, None, :] * values[:, 2:, :]
        + conv_taps[1][:, None, :] * values[:, 1:-1, :]
        + conv_taps[2][:, None, :] * values[:, :-2, :]
    )
    query = filtered[0]
    gated = filtered[1] * filtered[2]
    span = math.gcd(rows, 32)
    blocks = rows // span
    offsets = jnp.arange(span, dtype=jnp.float32)
    powers = jnp.exp(-decay_rate[None] * offsets[:, None, None])
    response = jnp.sum(residue[None] * powers, axis=1)
    lags = jnp.arange(span)[:, None] - jnp.arange(span)[None, :]
    toeplitz = jnp.where((lags >= 0)[:, :, None], response[jnp.clip(lags, 0, span - 1)], 0.0)
    blocked = gated.reshape(blocks, span, chans)
    inside = jnp.einsum("tsc,bsc->btc", toeplitz, blocked, precision=lax.Precision.HIGHEST)
    tails = jnp.exp(-decay_rate[None] * (span - 1.0 - offsets)[:, None, None])
    ends = jnp.einsum("spc,bsc->bpc", tails, blocked, precision=lax.Precision.HIGHEST)
    block_decay = jnp.broadcast_to(jnp.exp(-decay_rate * span)[None], ends.shape)
    after = lax.associative_scan(link, (block_decay, ends), axis=0)[1]
    final = after[blocks - 1]
    starts = jnp.concatenate([jnp.zeros_like(after[:1]), after[: blocks - 1]], axis=0)
    segment = jnp.exp(-decay_rate * rows)
    carried = entering(
        (segment, final), "ctx", link, (jnp.ones_like(final), jnp.zeros_like(final))
    )[1]
    block_starts = (span * jnp.arange(blocks, dtype=jnp.float32))[:, None, None]
    begin = starts + jnp.exp(-decay_rate[None] * block_starts) * carried[None]
    leading = residue[None] * jnp.exp(-decay_rate[None] * (offsets + 1.0)[:, None, None])
    convolved = inside + jnp.einsum("tpc,bpc->btc", leading, begin, precision=lax.Precision.HIGHEST)
    convolved = convolved.reshape(rows, chans)
    return (query * (convolved + skip[None, :] * gated)).astype(jnp.bfloat16)


def solution(mesh):
    placed = (
        P("ctx", "tp"),
        P("ctx", None, "tp"),
        P(None, None, "tp"),
        P(None, "tp"),
        P(None, "tp"),
        P("tp"),
    )
    return jax.shard_map(
        per_device, mesh=mesh, in_specs=placed, out_specs=P("ctx", "tp"), check_vma=False
    )
```

profile of v0, /device:TPU:32, one launch (start us, length us, event | category | flops | bytes accessed | tf_op | source)
XLA Modules:
  0.0 293.2 jit_solution(15202066247814389937)
XLA Ops:
  8.1 1.5 multiply_exponential_fusion
  10.4 24.7 %all-gather.6.cloned.1.call-done = bf16[128,4096]{1,0:T(8,128)(2,1)} async-done(((bf16[128,1024]{1,0:T(8,128)(2,1)}), bf16[128,4096]{1,0:T(8,128)(2,1)}) %all-gather.6.cloned.1.call-update) | async-done | bytes 1048592 | tf_op jit(solution)/shard_map/all_gather | solution.py:38
  35.1 94.1 %all-gather.8.cloned.1.call-done = bf16[4096,3,1024]{2,0,1:T(8,128)(2,1)} async-done(((bf16[128,3,1024]{2,0,1:T(8,128)(2,1)}), bf16[4096,3,1024]{2,0,1:T(8,128)(2,1)}) %all-gather.8.cloned.1.call-update) | async-done | bytes 25165840 | tf_op jit(solution)/shard_map/all_gather | solution.py:39
  129.2 5.0 %fusion.27 = bf16[1,128,1024]{2,1,0:T(8,128)(2,1)S(1)} fusion(bf16[128,4096]{1,0:T(8,128)(2,1)} %all-gather.6.cloned.1.call-done, bf16[4096,3,1024]{2,0,1:T(8,128)(2,1)} %all-gather.8.cloned.1.call-done), kind=kOutput, calls=%fused_computation.36 | convolution fusion | flops 1073872896 | bytes 9699328 | tf_op jit(solution)/shard_map/dot_general | solution.py:41
  134.1 4.6 %fusion.28 = bf16[1,128,1024]{2,1,0:T(8,128)(2,1)S(1)} fusion(bf16[128,4096]{1,0:T(8,128)(2,1)S(1)} %copy-done.15, bf16[4096,3,1024]{2,0,1:T(8,128)(2,1)} %all-gather.8.cloned.1.call-done), kind=kOutput, calls=%fused_computation.37 | convolution fusion | flops 1073872896 | bytes 9699328 | tf_op jit(solution)/shard_map/dot_general | solution.py:41
  138.8 4.7 %fusion.29 = bf16[1,128,1024]{2,1,0:T(8,128)(2,1)S(1)} fusion(bf16[128,4096]{1,0:T(8,128)(2,1)S(1)} %copy-done.15, bf16[4096,3,1024]{2,0,1:T(8,128)(2,1)} %all-gather.8.cloned.1.call-done), kind=kOutput, calls=%fused_computation.38 | convolution fusion | flops 1073872896 | bytes 9699328 | tf_op jit(solution)/shard_map/dot_general | solution.py:41
  143.5 2.4 collective-permute-start
  146.1 4.6 %collective-permute-done = bf16[3,2,1024]{2,1,0:T(2,128)(2,1)S(1)} collective-permute-done((bf16[3,2,1024]{2,1,0:T(2,128)(2,1)S(1)}, bf16[3,2,1024]{2,1,0:T(2,128)(2,1)S(1)}, u32[]{:S(2)}, u32[]{:S(2)}) %collective-permute-start) | collective-permute-done | bytes 12320 | tf_op jit(solution)/shard_map/ppermute | solution.py:11
  151.6 1.1 copy-done
  153.5 14.8 %fusion.10 = f32[1024,4,16]{2,1,0:T(4,128)} fusion(f32[4,32,1024]{1,0,2:T(4,128)S(1)} %copy.65, f32[32]{0:T(128)S(1)} %iota_subtract_fusion, f32[16,1024]{0,1:T(8,128)S(1)} %copy.62), kind=kOutput, calls=%fused_computation.16 | convolution fusion | flops 25690112 | bytes 852096 | tf_op jit(solution)/shard_map/spc,bsc->bpc/dot_general | solution.py:64
  168.4 1.9 copy.67
  171.1 1.0 copy.61
  172.2 15.3 %multiply_reduce_fusion = f32[32,1024]{0,1:T(8,128)S(1)} fusion(f32[16,1024]{0,1:T(8,128)S(1)} %copy.62, f32[16,1024]{0,1:T(8,128)} %copy.61), kind=kLoop, calls=%fused_computation.20 | loop fusion | flops 1540096 | bytes 262144 | tf_op jit(solution)/shard_map/reduce_sum | solution.py:58
  187.7 5.4 %gather_fusion = f32[1024,1024]{1,0:T(8,128)} fusion(f32[32,1024]{1,0:T(8,128)S(1)} %copy.63, s32[1024]{0:T(1024)S(1)} %broadcast_clamp_fusion), kind=kCustom, calls=%fused_computation | custom fusion | bytes 8392704 | tf_op jit(solution)/shard_map/gather | solution.py:60
  193.2 14.4 %copy.64 = f32[32,32,1024]{1,0,2:T(8,128)} copy(f32[32,32,1024]{2,1,0:T(8,128)} %bitcast.79) | data formatting | bytes 8388608 | tf_op jit(solution)/shard_map/gather | solution.py:60
  208.4 29.5 %fusion.1 = f32[1024,4,32]{2,1,0:T(4,128)} fusion(f32[4,32,1024]{1,0,2:T(4,128)S(1)} %copy.65, f32[32,32,1024]{1,0,2:T(8,128)} %copy.64, pred[32,32]{1,0:T(8,128)(4,1)S(1)} %subtract_compare_fusion), kind=kOutput, calls=%fused_computation.4 | convolution fusion | flops 51380224 | bytes 5243904 | tf_op jit(solution)/shard_map/tsc,bsc->btc/dot_general | solution.py:62
  238.0 30.1 %while.14 = (s32[]{:T(128)}, f32[16,1024]{1,0:T(8,128)S(1)}, s32[]{:T(128)}, f32[32,16,1024]{2,1,0:T(8,128)}, f32[32,16,1024]{2,1,0:T(8,128)}, /*index=5*/s32[]{:T(128)}, s32[]{:T(128)}) while((s32[]{:T(128)}, f32[16,1024]{1,0:T(8,128)S(1)}, s32[]{:T(128)}, f32[32,16,1024]{2,1,0:T(8,128)}, f32[32,16,1024]{2,1,0:T(8,128)}, ...), condition=%wide.region_2.3_spmd.clone, body=%wide.region_1.2_spmd.clone.sunk | while | flops 65540 | bytes 262253 | solution.py:28
  238.0 1.1 fusion.45
  243.8 0.9 fusion.45
  244.7 0.9 fusion.45
  268.1 1.0 multiply_add_fusion
  269.2 1.7 copy.68
  270.9 12.9 %add_bitcast_fusion = f32[4,32,1024]{1,0,2:T(4,128)} fusion(f32[1024,4,32]{2,1,0:T(4,128)S(1)} %copy-done.2, f32[4,16,1024]{1,0,2:T(4,128)} %copy.68, f32[32]{0:T(128)S(1)} %iota_add_fusion, f32[16,1024]{0,1:T(8,128)S(1)} %copy.62, f32[16,1024]{0,1:T(8,128)S(1)} %copy-done.3), kind=kOutput, calls=%fused_computation.27 | convolution fusion | flops 26345472 | bytes 1441920 | tf_op jit(solution)/shard_map/tpc,bpc->btc/dot_general | solution.py:76
  283.8 2.0 copy.69
  (98 shorter events, 33.7 us)
Async XLA Ops:
  6.5 28.5 %all-gather.6.cloned.1.call-start = ((), (), s32[]{:S(2)}) async-start(), calls=%async_computation | async-start | bytes 1310720 | tf_op jit(solution)/shard_map/all_gather | solution.py:38
  7.3 121.9 %all-gather.8.cloned.1.call-start = ((), (), s32[]{:S(2)}) async-start(), calls=%async_computation.1 | async-start | bytes 25952256 | tf_op jit(solution)/shard_map/all_gather | solution.py:39
  8.0 230.0 %all-gather.12.cloned.1.call-start = ((), (), s32[]{:S(2)}) async-start(), calls=%async_computation.3 | async-start | bytes 2162688 | tf_op jit(solution)/shard_map/all_gather | solution.py:16
  9.5 136.3 %copy-start.11 = (f32[16,1024]{1,0:T(8,128)}, f32[16,1024]{1,0:T(8,128)S(1)}, u32[]{:S(2)}) copy-start(f32[16,1024]{1,0:T(8,128)S(1)} %get-tuple-element.144) | copy-start | bytes 196612
  9.6 228.4 %all-gather.10.cloned.1.call-start = ((), (), s32[]{:S(2)}) async-start(), calls=%async_computation.2 | async-start | bytes 2162688 | tf_op jit(solution)/shard_map/all_gather | solution.py:16
  35.1 99.1 %copy-start.15 = (bf16[128,4096]{1,0:T(8,128)(2,1)S(1)}, bf16[128,4096]{1,0:T(8,128)(2,1)}, u32[]{:S(2)}) copy-start(bf16[128,4096]{1,0:T(8,128)(2,1)} %all-gather.6.cloned.1.call-done) | copy-start | bytes 3145732
  143.5 7.2 %collective-permute-start = (bf16[3,2,1024]{2,1,0:T(2,128)(2,1)S(1)}, bf16[3,2,1024]{2,1,0:T(2,128)(2,1)S(1)}, u32[]{:S(2)}, u32[]{:S(2)}) collective-permute-start(bf16[3,2,1024]{2,1,0:T(2,128)(2,1)S(1)} %pad_maximum_fusion.1), channel_id=1, source_target_pairs={{0,4},{4,8},{8,12},{12,16},{16,20},{20,24},{24,28},{28,32},{32,36}... | collective-permute-start | bytes 36872 | tf_op jit(solution)/shard_map/ppermute | solution.py:11
  151.6 1.1 copy-start
  168.4 1.9 copy-start.6
  168.4 2.7 copy-start.13
  170.3 0.8 copy-start.4
  170.4 0.7 copy-start.7
  170.4 0.8 copy-start.9
  193.1 14.5 %copy-start.5 = (f32[1024,4,16]{0,2,1:T(8,128)S(1)}, f32[1024,4,16]{0,2,1:T(8,128)}, u32[]{:S(2)}) copy-start(f32[1024,4,16]{0,2,1:T(8,128)} %copy-done.4) | copy-start | bytes 786436
  193.1 14.5 %copy-start.8 = (f32[1,16,1024]{2,1,0:T(8,128)S(1)}, f32[1,16,1024]{2,1,0:T(8,128)}, u32[]{:S(2)}) copy-start(f32[1,16,1024]{2,1,0:T(8,128)} %copy-done.7) | copy-start | bytes 196612
  193.1 14.5 %copy-start.10 = (f32[1,16,1024]{2,1,0:T(8,128)S(1)}, f32[1,16,1024]{2,1,0:T(8,128)}, u32[]{:S(2)}) copy-start(f32[1,16,1024]{2,1,0:T(8,128)} %copy-done.9) | copy-start | bytes 196612
  208.4 59.7 %copy-start.12 = (f32[16,1024]{1,0:T(8,128)S(1)}, f32[16,1024]{1,0:T(8,128)}, u32[]{:S(2)}) copy-start(f32[16,1024]{1,0:T(8,128)} %copy-done.11) | copy-start | bytes 196612
  238.0 32.9 %copy-start.2 = (f32[1024,4,32]{2,1,0:T(4,128)S(1)}, f32[1024,4,32]{2,1,0:T(4,128)}, u32[]{:S(2)}) copy-start(f32[1024,4,32]{2,1,0:T(4,128)} %fusion.1) | copy-start | bytes 1572868
  238.0 32.9 %copy-start.3 = (f32[16,1024]{0,1:T(8,128)S(1)}, f32[16,1024]{0,1:T(8,128)}, u32[]{:S(2)}) copy-start(f32[16,1024]{0,1:T(8,128)} %copy.61) | copy-start | bytes 196612
  283.8 2.0 copy-start.1
  283.8 2.0 copy-start.14
Sparse Core Ops, SparseCore 0:
  9.0 25.9 all-gather.5
  37.4 91.7 all-gather.7
  131.4 43.6 all-gather.11
  177.3 43.2 all-gather.9
where the time goes:
time: 295 us; the launch traced here: 293 us
  waiting for transfers between devices  125 us (42%)
  matrix products  71.5 us (24%)
  other arithmetic  49.9 us (17%)
  local copies, waits for them, and re-layouts  30.4 us (10%)
  between operations  13.5 us (5%)
    all_gather x1, waiting for transfers between devices, per_device(): piece = lax.all_gather(in_weight, 'ctx', axis=0, tiled=True)  94.1 us
    dot_general x1, matrix products, per_device(): jnp.einsum('tsc,bsc->btc', toeplitz, blocked, precision=lax.Precision.HIG...  29.5 us
    select_n x32, other arithmetic, turn(): return jax.tree.map(lambda a, b: jnp.where(reached, a, b), new, before)  29.4 us
    all_gather x1, waiting for transfers between devices, per_device(): whole = lax.all_gather(tokens, 'tp', axis=1, tiled=True)  24.7 us
    gather x2, local copies, waits for them, and re-layouts, per_device(): response[jnp.clip(lags, 0, span - 1)]  19.8 us
    reduce_sum x1, other arithmetic, per_device(): response = jnp.sum(residue[None] * powers, axis=1)  15.3 us
    dot_general x1, matrix products, per_device(): jnp.einsum('spc,bsc->bpc', tails, blocked, precision=lax.Precision.HIGHEST)  14.8 us
    dot_general x3, matrix products, per_device(): jnp.dot(whole, piece[:, g, :], preferred_element_type=jnp.float32)  14.3 us
  transfers between devices with their start and end apart: 5, of which 3 were waited for; matrix products, arithmetic and copies ran while one was open for 35% of the time, Pallas kernels for 0%

commit v1 on v0

--- a/solution.py
+++ b/solution.py
@@ -35,7 +35,12 @@
 def per_device(tokens, in_weight, conv_taps, decay_rate, residue, skip):
     rows = tokens.shape[0]
     chans = in_weight.shape[2]
-    whole = lax.all_gather(tokens, "tp", axis=1, tiled=True)
+    ring = [tokens]
+    for hop in range(3):
+        ring.append(lax.ppermute(ring[-1], "tp", [(dev, (dev + 1) % 4) for dev in range(4)]))
+    whole = jnp.roll(
+        jnp.concatenate(ring[::-1], axis=1), (lax.axis_index("tp") + 1) * ring[0].shape[1], axis=1
+    )
     piece = lax.all_gather(in_weight, "ctx", axis=0, tiled=True)
     sums = tuple(
         (jnp.dot(whole, piece[:, g, :], preferred_element_type=jnp.float32) for g in range(3))

time: 295 us -> 270 us (0.915)
  waiting for transfers between devices: 125 us -> 90.9 us
  local copies, waits for them, and re-layouts: 30.4 us -> 36.4 us
    all_gather x1, waiting for transfers between devices: 94.1 us -> 64.3 us  [per_device(): piece = lax.all_gather(in_weight, 'ctx', axis=0, tiled=True)]
    all_gather x1 -> x0, waiting for transfers between devices: 24.7 us -> none  [per_device(): whole = lax.all_gather(tokens, 'tp', axis=1, tiled=True)]
    ppermute x0 -> x3, waiting for transfers between devices: none -> 21.3 us  [per_device(): lax.ppermute(ring[-1], 'tp', [(dev, (dev + 1) % 4) for dev in range(4)])]
    unnamed x34 -> x41, local copies, waits for them, and re-layouts: 2.25 us -> 7.44 us
  transfers between devices with their start and end apart: 5 -> 7, of which waited for: 3 -> 5; matrix products, arithmetic and copies ran while one was open for 35% -> 41% of each run, Pallas kernels for 0% -> 0%
where the time goes in v1:
time: 270 us; the launch traced here: 268 us
  waiting for transfers between devices  90.9 us (34%)
  matrix products  72.2 us (27%)
  other arithmetic  49.9 us (18%)
  local copies, waits for them, and re-layouts  36.4 us (13%)
  between operations  13.5 us (5%)
  starting transfers between devices  4.39 us (2%)
    all_gather x1, waiting for transfers between devices, per_device(): piece = lax.all_gather(in_weight, 'ctx', axis=0, tiled=True)  64.3 us
    dot_general x1, matrix products, per_device(): jnp.einsum('tsc,bsc->btc', toeplitz, blocked, precision=lax.Precision.HIG...  29.5 us
    select_n x32, other arithmetic, turn(): return jax.tree.map(lambda a, b: jnp.where(reached, a, b), new, before)  29.4 us
    ppermute x3, waiting for transfers between devices, per_device(): lax.ppermute(ring[-1], 'tp', [(dev, (dev + 1) % 4) for dev in range(4)])  21.3 us
    gather x2, local copies, waits for them, and re-layouts, per_device(): response[jnp.clip(lags, 0, span - 1)]  19.8 us
    reduce_sum x1, other arithmetic, per_device(): response = jnp.sum(residue[None] * powers, axis=1)  15.3 us
    dot_general x3, matrix products, per_device(): jnp.dot(whole, piece[:, g, :], preferred_element_type=jnp.float32)  15 us
    dot_general x1, matrix products, per_device(): jnp.einsum('spc,bsc->bpc', tails, blocked, precision=lax.Precision.HIGHEST)  14.8 us
  transfers between devices with their start and end apart: 7, of which 5 were waited for; matrix products, arithmetic and copies ran while one was open for 41% of the time, Pallas kernels for 0%

profile of v1, /device:TPU:32, one launch (start us, length us, event | category | flops | bytes accessed | tf_op | source)
XLA Modules:
  0.0 268.0 jit_solution(16639440447974538050)
XLA Ops:
  7.3 1.6 collective-permute-start
  8.9 8.0 %collective-permute-done = bf16[128,1024]{1,0:T(8,128)(2,1)S(1)} collective-permute-done((bf16[128,1024]{1,0:T(8,128)(2,1)}, bf16[128,1024]{1,0:T(8,128)(2,1)S(1)}, u32[]{:S(2)}, u32[]{:S(2)}) %collective-permute-start) | collective-permute-done | bytes 262176 | tf_op jit(solution)/shard_map/ppermute | solution.py:40
  17.2 8.2 %collective-permute-done.1 = bf16[128,1024]{1,0:T(8,128)(2,1)S(1)} collective-permute-done((bf16[128,1024]{1,0:T(8,128)(2,1)S(1)}, bf16[128,1024]{1,0:T(8,128)(2,1)S(1)}, u32[]{:S(2)}, u32[]{:S(2)}) %collective-permute-start.1) | collective-permute-done | bytes 262176 | tf_op jit(solution)/shard_map/ppermute | solution.py:40
  25.4 1.5 multiply_exponential_fusion
  27.7 5.2 %collective-permute-done.2 = bf16[128,1024]{1,0:T(8,128)(2,1)S(1)} collective-permute-done((bf16[128,1024]{1,0:T(8,128)(2,1)S(1)}, bf16[128,1024]{1,0:T(8,128)(2,1)S(1)}, u32[]{:S(2)}, u32[]{:S(2)}) %collective-permute-start.2) | collective-permute-done | bytes 262176 | tf_op jit(solution)/shard_map/ppermute | solution.py:40
  38.9 64.3 %all-gather.5.cloned.1.call-done = bf16[4096,3,1024]{2,0,1:T(8,128)(2,1)} async-done(((bf16[128,3,1024]{2,0,1:T(8,128)(2,1)}), bf16[4096,3,1024]{2,0,1:T(8,128)(2,1)}) %all-gather.5.cloned.1.call-update) | async-done | bytes 25165840 | tf_op jit(solution)/shard_map/all_gather | solution.py:44
  103.2 5.0 %fusion.29 = bf16[1,128,1024]{2,1,0:T(8,128)(2,1)S(1)} fusion(bf16[4096,3,1024]{2,0,1:T(8,128)(2,1)} %all-gather.5.cloned.1.call-done, bf16[128,8192]{1,0:T(8,128)(2,1)} %constant_dynamic-update-slice_fusion, s32[]{:T(128)S(6)} %select_n.50), kind=kOutput, calls=%fused_computation.38 | convolution fusion | flops 1073872896 | bytes 9699332 | tf_op jit(solution)/shard_map/dot_general | solution.py:46
  108.2 5.0 %fusion.28 = bf16[1,128,1024]{2,1,0:T(8,128)(2,1)S(1)} fusion(bf16[4096,3,1024]{2,0,1:T(8,128)(2,1)} %all-gather.5.cloned.1.call-done, bf16[128,8192]{1,0:T(8,128)(2,1)} %constant_dynamic-update-slice_fusion, s32[]{:T(128)S(6)} %select_n.50), kind=kOutput, calls=%fused_computation.37 | convolution fusion | flops 1073872896 | bytes 9699332 | tf_op jit(solution)/shard_map/dot_general | solution.py:46
  113.1 5.1 %fusion.27 = bf16[1,128,1024]{2,1,0:T(8,128)(2,1)S(1)} fusion(bf16[4096,3,1024]{2,0,1:T(8,128)(2,1)} %all-gather.5.cloned.1.call-done, bf16[128,8192]{1,0:T(8,128)(2,1)} %constant_dynamic-update-slice_fusion, s32[]{:T(128)S(6)} %select_n.50), kind=kOutput, calls=%fused_computation.36 | convolution fusion | flops 1073872896 | bytes 9699332 | tf_op jit(solution)/shard_map/dot_general | solution.py:46
  118.2 2.4 collective-permute-start.3
  120.8 4.5 %collective-permute-done.3 = bf16[3,2,1024]{2,1,0:T(2,128)(2,1)S(1)} collective-permute-done((bf16[3,2,1024]{2,1,0:T(2,128)(2,1)S(1)}, bf16[3,2,1024]{2,1,0:T(2,128)(2,1)S(1)}, u32[]{:S(2)}, u32[]{:S(2)}) %collective-permute-start.3) | collective-permute-done | bytes 12320 | tf_op jit(solution)/shard_map/ppermute | solution.py:11
  126.3 1.1 copy-done
  128.2 14.8 %fusion.10 = f32[1024,4,16]{2,1,0:T(4,128)} fusion(f32[4,32,1024]{1,0,2:T(4,128)S(1)} %copy.65, f32[32]{0:T(128)S(1)} %iota_subtract_fusion, f32[16,1024]{0,1:T(8,128)S(1)} %copy.62), kind=kOutput, calls=%fused_computation.16 | convolution fusion | flops 25690112 | bytes 852096 | tf_op jit(solution)/shard_map/spc,bsc->bpc/dot_general | solution.py:69
  143.1 2.0 copy.67
  146.9 15.3 %multiply_reduce_fusion = f32[32,1024]{0,1:T(8,128)S(1)} fusion(f32[16,1024]{0,1:T(8,128)S(1)} %copy.62, f32[16,1024]{0,1:T(8,128)} %copy.61), kind=kLoop, calls=%fused_computation.20 | loop fusion | flops 1540096 | bytes 262144 | tf_op jit(solution)/shard_map/reduce_sum | solution.py:63
  162.5 5.4 %gather_fusion = f32[1024,1024]{1,0:T(8,128)} fusion(f32[32,1024]{1,0:T(8,128)S(1)} %copy.63, s32[1024]{0:T(1024)S(1)} %broadcast_clamp_fusion), kind=kCustom, calls=%fused_computation | custom fusion | bytes 8392704 | tf_op jit(solution)/shard_map/gather | solution.py:65
  167.9 14.4 %copy.64 = f32[32,32,1024]{1,0,2:T(8,128)} copy(f32[32,32,1024]{2,1,0:T(8,128)} %bitcast.76) | data formatting | bytes 8388608 | tf_op jit(solution)/shard_map/gather | solution.py:65
  183.2 29.5 %fusion.1 = f32[1024,4,32]{2,1,0:T(4,128)} fusion(f32[4,32,1024]{1,0,2:T(4,128)S(1)} %copy.65, f32[32,32,1024]{1,0,2:T(8,128)} %copy.64, pred[32,32]{1,0:T(8,128)(4,1)S(1)} %subtract_compare_fusion), kind=kOutput, calls=%fused_computation.4 | convolution fusion | flops 51380224 | bytes 5243904 | tf_op jit(solution)/shard_map/tsc,bsc->btc/dot_general | solution.py:67
  212.8 30.1 %while.14 = (s32[]{:T(128)}, f32[16,1024]{1,0:T(8,128)S(1)}, s32[]{:T(128)}, f32[32,16,1024]{2,1,0:T(8,128)}, f32[32,16,1024]{2,1,0:T(8,128)}, /*index=5*/s32[]{:T(128)}, s32[]{:T(128)}) while((s32[]{:T(128)}, f32[16,1024]{1,0:T(8,128)S(1)}, s32[]{:T(128)}, f32[32,16,1024]{2,1,0:T(8,128)}, f32[32,16,1024]{2,1,0:T(8,128)}, ...), condition=%wide.region_2.3_spmd.clone, body=%wide.region_1.2_spmd.clone.sunk | while | flops 65540 | bytes 262245 | solution.py:28
  212.8 1.1 fusion.48
  242.9 1.0 multiply_add_fusion
  244.0 1.7 copy.68
  245.7 12.9 %add_bitcast_fusion = f32[4,32,1024]{1,0,2:T(4,128)} fusion(f32[1024,4,32]{2,1,0:T(4,128)S(1)} %copy-done.2, f32[4,16,1024]{1,0,2:T(4,128)} %copy.68, f32[32]{0:T(128)S(1)} %iota_add_fusion, f32[16,1024]{0,1:T(8,128)S(1)} %copy.62, f32[16,1024]{0,1:T(8,128)S(1)} %copy-done.3), kind=kOutput, calls=%fused_computation.27 | convolution fusion | flops 26345472 | bytes 1441920 | tf_op jit(solution)/shard_map/tpc,bpc->btc/dot_general | solution.py:81
  258.6 2.0 copy.69
  (109 shorter events, 42.0 us)
Async XLA Ops:
  6.5 28.7 %copy-start.6 = (bf16[128,1024]{1,0:T(8,128)(2,1)S(1)}, bf16[128,1024]{1,0:T(8,128)(2,1)}, u32[]{:S(2)}) copy-start(bf16[128,1024]{1,0:T(8,128)(2,1)} %param.8) | copy-start | bytes 786436
  6.5 96.6 %all-gather.5.cloned.1.call-start = ((), (), s32[]{:S(2)}) async-start(), calls=%async_computation | async-start | bytes 25952256 | tf_op jit(solution)/shard_map/all_gather | solution.py:44
  7.3 205.5 %all-gather.9.cloned.1.call-start = ((), (), s32[]{:S(2)}) async-start(), calls=%async_computation.2 | async-start | bytes 2162688 | tf_op jit(solution)/shard_map/all_gather | solution.py:16
  7.3 9.6 %collective-permute-start = (bf16[128,1024]{1,0:T(8,128)(2,1)}, bf16[128,1024]{1,0:T(8,128)(2,1)S(1)}, u32[]{:S(2)}, u32[]{:S(2)}) collective-permute-start(bf16[128,1024]{1,0:T(8,128)(2,1)} %param.8), channel_id=1, source_target_pairs={{0,1},{1,2},{2,3},{3,0},{4,5},{5,6},{6,7},{7,4},{8,9},{9,10},{10,1... | collective-permute-start | bytes 786440 | tf_op jit(solution)/shard_map/ppermute | solution.py:40
  16.9 8.5 %collective-permute-start.1 = (bf16[128,1024]{1,0:T(8,128)(2,1)S(1)}, bf16[128,1024]{1,0:T(8,128)(2,1)S(1)}, u32[]{:S(2)}, u32[]{:S(2)}) collective-permute-start(bf16[128,1024]{1,0:T(8,128)(2,1)S(1)} %collective-permute-done), channel_id=1, source_target_pairs={{0,1},{1,2},{2,3},{3,0},{4,5},{5,6},{6,7},{7,4},{8,9},{9,10},{10,1... | collective-permute-start | bytes 786440 | tf_op jit(solution)/shard_map/ppermute | solution.py:40
  25.4 7.6 %collective-permute-start.2 = (bf16[128,1024]{1,0:T(8,128)(2,1)S(1)}, bf16[128,1024]{1,0:T(8,128)(2,1)S(1)}, u32[]{:S(2)}, u32[]{:S(2)}) collective-permute-start(bf16[128,1024]{1,0:T(8,128)(2,1)S(1)} %collective-permute-done.1), channel_id=1, source_target_pairs={{0,1},{1,2},{2,3},{3,0},{4,5},{5,6},{6,7},{7,4},{8,9},{9,10},{10,1... | collective-permute-start | bytes 786440 | tf_op jit(solution)/shard_map/ppermute | solution.py:40
  26.8 93.8 %copy-start.12 = (f32[16,1024]{1,0:T(8,128)}, f32[16,1024]{1,0:T(8,128)S(1)}, u32[]{:S(2)}) copy-start(f32[16,1024]{1,0:T(8,128)S(1)} %get-tuple-element.144) | copy-start | bytes 196612
  26.9 185.9 %all-gather.7.cloned.1.call-start = ((), (), s32[]{:S(2)}) async-start(), calls=%async_computation.1 | async-start | bytes 2162688 | tf_op jit(solution)/shard_map/all_gather | solution.py:16
  118.2 7.1 %collective-permute-start.3 = (bf16[3,2,1024]{2,1,0:T(2,128)(2,1)S(1)}, bf16[3,2,1024]{2,1,0:T(2,128)(2,1)S(1)}, u32[]{:S(2)}, u32[]{:S(2)}) collective-permute-start(bf16[3,2,1024]{2,1,0:T(2,128)(2,1)S(1)} %pad_maximum_fusion.1), channel_id=1, source_target_pairs={{0,4},{4,8},{8,12},{12,16},{16,20},{20,24},{24,28},{28,32},{32,36}... | collective-permute-start | bytes 36872 | tf_op jit(solution)/shard_map/ppermute | solution.py:11
  126.2 1.1 copy-start
  143.1 2.0 copy-start.7
  143.1 2.8 %copy-start.14 = (f32[16,1024]{1,0:T(8,128)S(1)}, f32[16,1024]{1,0:T(8,128)}, u32[]{:S(2)}) copy-start(f32[16,1024]{1,0:T(8,128)} %param.12) | copy-start | bytes 196612
  145.1 0.8 copy-start.4
  145.1 0.7 copy-start.8
  145.1 0.8 copy-start.10
  167.9 14.5 %copy-start.5 = (f32[1024,4,16]{0,2,1:T(8,128)S(1)}, f32[1024,4,16]{0,2,1:T(8,128)}, u32[]{:S(2)}) copy-start(f32[1024,4,16]{0,2,1:T(8,128)} %copy-done.4) | copy-start | bytes 786436
  167.9 14.5 %copy-start.9 = (f32[1,16,1024]{2,1,0:T(8,128)S(1)}, f32[1,16,1024]{2,1,0:T(8,128)}, u32[]{:S(2)}) copy-start(f32[1,16,1024]{2,1,0:T(8,128)} %copy-done.8) | copy-start | bytes 196612
  167.9 14.5 %copy-start.11 = (f32[1,16,1024]{2,1,0:T(8,128)S(1)}, f32[1,16,1024]{2,1,0:T(8,128)}, u32[]{:S(2)}) copy-start(f32[1,16,1024]{2,1,0:T(8,128)} %copy-done.10) | copy-start | bytes 196612
  183.2 59.7 %copy-start.13 = (f32[16,1024]{1,0:T(8,128)S(1)}, f32[16,1024]{1,0:T(8,128)}, u32[]{:S(2)}) copy-start(f32[16,1024]{1,0:T(8,128)} %copy-done.12) | copy-start | bytes 196612
  212.8 32.9 %copy-start.2 = (f32[1024,4,32]{2,1,0:T(4,128)S(1)}, f32[1024,4,32]{2,1,0:T(4,128)}, u32[]{:S(2)}) copy-start(f32[1024,4,32]{2,1,0:T(4,128)} %fusion.1) | copy-start | bytes 1572868
  212.8 32.9 %copy-start.3 = (f32[16,1024]{0,1:T(8,128)S(1)}, f32[16,1024]{0,1:T(8,128)}, u32[]{:S(2)}) copy-start(f32[16,1024]{0,1:T(8,128)} %copy.61) | copy-start | bytes 196612
  258.6 2.0 copy-start.1
  258.6 2.0 copy-start.15
Sparse Core Ops, SparseCore 0:
  9.7 93.4 all-gather.4
  105.4 43.7 all-gather.8
  151.5 43.2 all-gather.6
